TPU v7x, 32 devices: a whole 2x2x4 slice. The times are simulated.
32 devices in a mesh: groups: 2 (over y), var: 4 (over z), probe: 2 (over x), rep: 2 (over core).
Axes of the slice: x: 2, y: 2, z: 4, core: 2. Of those that a mesh axis runs over, the one named last changes fastest.
Arguments:
- block_values: bfloat16 [512, 6, 128, 128], P(('groups', 'var'), 'rep'), parts along dimension 0, may hold values from -6 to 6
- columns: int32 [512, 6], P(('groups', 'var'), 'rep'), parts along dimension 0, may hold values from 0 to 255, as said below
- probe_signs: int32 [512, 24, 128], P('groups', 'probe'), parts along dimension 0, may hold values from -1 to 1, as said below
Outputs:
- gradient: bfloat16 [512, 6, 128, 128], P(('groups', 'var'), 'rep'), parts along dimension 0
There are 2 independent parts, one for each index of `groups`. A program takes and returns all parts, laid end to end along the dimension named above; each array names one. Nothing has to cross between parts.
Inputs may be any that keep to these rules, and one draw needn't show every extreme that they name: The 6 block columns of each block row are distinct. `probe_signs`: every entry is -1 or 1.
All inputs are finite; a program needn't handle non-finite values.
Results may differ from a plain program's by a relative error of at most 0.015.
Values may be sent and summed in bfloat16 or wider, within the bound.
No kernel may reach another device: no remote copies, remote signals or barrier semaphores. Data moves between devices by JAX's collectives and lax.ppermute only.
A program may use at most 128 MiB of HBM per device.

v0:
```python
import math
import jax
import jax.numpy as jnp
from jax import lax
from jax.sharding import PartitionSpec as P

BLK = 128
KS = 6


def local(block_values, columns, probe_signs):
    rows_here = block_values.shape[0]
    slots_here = block_values.shape[1]
    block_width = block_values.shape[3]
    blocks_all = probe_signs.shape[0]
    probes_here = probe_signs.shape[1]
    inverse = 1.0 / math.sqrt(KS * BLK)
    column_list = columns.reshape(-1)
    total_probes = probes_here * lax.axis_size("probe")
    signs_all = probe_signs.astype(jnp.bfloat16)
    own_rows = lax.dynamic_slice_in_dim(signs_all, lax.axis_index("var") * rows_here, rows_here, 0)

    def select_local(panel_all):
        return jnp.take(panel_all, column_list, axis=0)

    forward_blocks = [select_local(signs_all)]
    back_panels = [own_rows]
    forward_own = own_rows
    for step_index in range(3):
        shaped = forward_blocks[step_index].reshape(rows_here, slots_here, probes_here, block_width)
        product = jnp.einsum(
            "rkij,rksj->rsi", block_values, shaped, preferred_element_type=jnp.float32
        )
        product = lax.psum(product.astype(jnp.bfloat16), "rep").astype(jnp.float32)
        forward_own = (forward_own.astype(jnp.float32) + inverse * product).astype(jnp.bfloat16)
        forward_blocks.append(select_local(lax.all_gather(forward_own, "var", axis=0, tiled=True)))
    for step_index in range(3):
        panel_own = back_panels[step_index]
        weighted = jnp.einsum(
            "rkij,rsi->rksj", block_values, panel_own, preferred_element_type=jnp.float32
        )
        weighted = weighted.reshape(-1, probes_here, block_width)
        contrib = jax.ops.segment_sum(weighted, column_list, num_segments=blocks_all)
        share_rows = blocks_all // (lax.axis_size("var") * lax.axis_size("rep"))
        summed = lax.psum_scatter(
            contrib.astype(jnp.bfloat16), ("var", "rep"), scatter_dimension=0, tiled=True
        ).astype(jnp.float32)
        previous = lax.dynamic_slice_in_dim(
            panel_own, lax.axis_index("rep") * share_rows, share_rows, 0
        )
        updated = (previous.astype(jnp.float32) + inverse * summed).astype(jnp.bfloat16)
        back_panels.append(lax.all_gather(updated, "rep", axis=0, tiled=True))
    left_panels = jnp.stack(back_panels)
    right_blocks = jnp.stack(forward_blocks[::-1]).reshape(
        4, rows_here, slots_here, probes_here, block_width
    )
    estimate = jnp.einsum(
        "trsi,trksj->rkij", left_panels, right_blocks, preferred_element_type=jnp.float32
    )
    estimate = lax.psum(estimate.astype(jnp.bfloat16), "probe").astype(jnp.float32)
    return (estimate / total_probes).astype(jnp.bfloat16)


def solution(mesh):
    return jax.shard_map(
        local,
        mesh=mesh,
        in_specs=(
            P(("groups", "var"), "rep", None, None),
            P(("groups", "var"), "rep"),
            P("groups", "probe", None),
        ),
        out_specs=P(("groups", "var"), "rep", None, None),
        check_vma=False,
    )
```

profile of v0, /device:TPU:0, one launch (start us, length us, event | category | flops | bytes accessed | tf_op | source)
XLA Modules:
  0.0 377.1 jit_solution(8192982231538396565)
XLA Ops:
  7.4 0.8 copy.88
  8.1 0.1 reshape.35
  8.3 1.6 convert_element_type.87
  9.9 0.5 copy.89
  10.4 0.8 gather_fusion
  11.2 0.3 broadcast_select_fusion.2
  11.5 5.4 %convolution_bitcast_fusion.2 = bf16[64,12,128]{2,1,0:T(8,128)(2,1)S(1)} fusion(bf16[64,3,12,128]{3,2,1,0:T(8,128)(2,1)S(1)} %bitcast.66, bf16[64,3,128,128]{3,2,1,0:T(8,128)(2,1)} %param.5), kind=kOutput, calls=%fused_computation.22 | convolution fusion | flops 75497472 | bytes 7077888 | tf_op jit(solution)/shard_map/rkij,rksj->rsi/dot_general | solution.py:31
  16.9 0.7 copy.163
  17.6 0.0 reduce-scatter.4.cloned.1.call-start
  17.7 0.7 dynamic-slice_bitcast_fusion.1
  18.4 5.1 %fusion.18 = f32[64,12,3,128]{3,1,2,0:T(8,128)} fusion(bf16[64,3,128,128]{3,2,1,0:T(8,128)(2,1)} %param.5, bf16[64,12,128,1]{2,0,1,3:T(8,128)(2,1)S(1)} %get-tuple-element.7), kind=kOutput, calls=%fused_computation.44 | convolution fusion | flops 75497472 | bytes 7667712 | tf_op jit(solution)/shard_map/rkij,rsi->rksj/dot_general | solution.py:39
  23.6 0.1 broadcast.14.clone.1
  23.7 15.5 %scatter_fusion = f32[256,12,128]{2,1,0:T(8,128)S(1)} fusion(f32[256,12,128]{2,1,0:T(8,128)S(1)} %broadcast.14.clone.1, s32[192]{0:T(256)S(1)} %reshape.35, f32[192,12,128]{2,1,0:T(8,128)} %bitcast.64), kind=kCustom, calls=%fused_computation.4 | custom fusion | flops 294912 | bytes 3539712 | tf_op jit(solution)/shard_map/scatter-add | solution.py:43
  39.2 1.4 copy.160
  40.6 0.0 all-reduce.7.cloned.1.call-start
  40.7 1.0 add_convert_fusion.2
  41.7 24.9 %all_gather.18 = bf16[256,12,128]{2,0,1:T(8,128)(2,1)S(1)} all-gather(bf16[64,12,128]{2,0,1:T(8,128)(2,1)S(1)} %add_convert_fusion.2), channel_id=1, replica_groups=mesh['groups'=2,'var'=4,'probe'=2,'rep'=2] {'var'}, dimensions={0}, use_global_device_ids=true | all-gather | bytes 983040 | tf_op jit(solution)/shard_map/all_gather | solution.py:36
  66.6 0.5 copy.93
  67.2 0.8 gather_fusion.1
  68.0 0.3 broadcast_select_fusion.1
  68.2 5.4 %convolution_bitcast_fusion.1 = bf16[64,12,128]{2,1,0:T(8,128)(2,1)S(1)} fusion(bf16[64,3,12,128]{3,2,1,0:T(8,128)(2,1)S(1)} %bitcast.68, bf16[64,3,128,128]{3,2,1,0:T(8,128)(2,1)} %param.5), kind=kOutput, calls=%fused_computation.21 | convolution fusion | flops 75497472 | bytes 7077888 | tf_op jit(solution)/shard_map/rkij,rksj->rsi/dot_general | solution.py:31
  73.6 0.7 copy.162
  74.4 0.0 reduce-scatter.6.cloned.1.call-start
  74.5 2.3 reduce-scatter.4.cloned.1.call-done
  76.7 0.9 add_convert_fusion.5
  77.7 1.9 all_gather.21
  79.6 5.3 %fusion.16 = f32[64,12,3,128]{3,1,2,0:T(8,128)} fusion(bf16[64,3,128,128]{3,2,1,0:T(8,128)(2,1)} %param.5, bf16[64,12,128,1]{2,0,1,3:T(8,128)(2,1)S(1)} %bitcast.72), kind=kOutput, calls=%fused_computation.42 | convolution fusion | flops 75497472 | bytes 7667712 | tf_op jit(solution)/shard_map/rkij,rsi->rksj/dot_general | solution.py:39
  84.9 0.1 broadcast.14.clone
  85.1 15.5 %scatter_fusion.1 = f32[256,12,128]{2,1,0:T(8,128)S(1)} fusion(f32[256,12,128]{2,1,0:T(8,128)S(1)} %broadcast.14.clone, s32[192]{0:T(256)S(1)} %reshape.35, f32[192,12,128]{2,1,0:T(8,128)} %bitcast.65), kind=kCustom, calls=%fused_computation.5 | custom fusion | flops 294912 | bytes 3539712 | tf_op jit(solution)/shard_map/scatter-add | solution.py:43
  100.5 1.4 copy.159
  102.0 0.0 all-reduce.9.cloned.1.call-start
  102.0 0.0 all-reduce.7.cloned.1.call-done
  102.0 1.0 add_convert_fusion.1
  103.0 23.0 %all_gather.19 = bf16[256,12,128]{2,0,1:T(8,128)(2,1)S(1)} all-gather(bf16[64,12,128]{2,0,1:T(8,128)(2,1)S(1)} %add_convert_fusion.1), channel_id=1, replica_groups=mesh['groups'=2,'var'=4,'probe'=2,'rep'=2] {'var'}, dimensions={0}, use_global_device_ids=true | all-gather | bytes 983040 | tf_op jit(solution)/shard_map/all_gather | solution.py:36
  126.1 0.5 copy.97
  126.6 0.8 gather_fusion.2
  127.4 0.3 broadcast_select_fusion
  127.7 5.1 %convolution_bitcast_fusion = bf16[64,12,128]{2,1,0:T(8,128)(2,1)S(1)} fusion(bf16[64,3,12,128]{3,2,1,0:T(8,128)(2,1)S(1)} %bitcast.70, bf16[64,3,128,128]{3,2,1,0:T(8,128)(2,1)} %param.5), kind=kOutput, calls=%fused_computation.20 | convolution fusion | flops 75497472 | bytes 7077888 | tf_op jit(solution)/shard_map/rkij,rksj->rsi/dot_general | solution.py:31
  132.8 0.7 copy.161
  133.5 0.0 reduce-scatter.8.cloned.1.call-start
  133.6 0.4 reduce-scatter.6.cloned.1.call-done
  134.0 0.9 add_convert_fusion.4
  134.9 1.9 all_gather.22
  136.8 5.3 %fusion.14 = f32[64,12,3,128]{3,1,2,0:T(8,128)} fusion(bf16[64,3,128,128]{3,2,1,0:T(8,128)(2,1)} %param.5, bf16[64,12,128,1]{2,0,1,3:T(8,128)(2,1)S(1)} %bitcast.73), kind=kOutput, calls=%fused_computation.40 | convolution fusion | flops 75497472 | bytes 7667712 | tf_op jit(solution)/shard_map/rkij,rsi->rksj/dot_general | solution.py:39
  142.1 0.1 broadcast.14
  142.3 15.5 %scatter_fusion.2 = f32[256,12,128]{2,1,0:T(8,128)S(1)} fusion(f32[256,12,128]{2,1,0:T(8,128)S(1)} %broadcast.14, s32[192]{0:T(256)S(1)} %reshape.35, f32[192,12,128]{2,1,0:T(8,128)} %bitcast.63), kind=kCustom, calls=%fused_computation.6 | custom fusion | flops 294912 | bytes 3539712 | tf_op jit(solution)/shard_map/scatter-add | solution.py:43
  157.8 1.4 copy.158
  159.2 0.0 all-reduce.11.cloned.1.call-start
  159.3 0.8 copy.119
  160.1 1.0 add_convert_fusion
  161.1 22.7 %all_gather.20 = bf16[256,12,128]{2,0,1:T(8,128)(2,1)S(1)} all-gather(bf16[64,12,128]{2,0,1:T(8,128)(2,1)S(1)} %add_convert_fusion), channel_id=1, replica_groups=mesh['groups'=2,'var'=4,'probe'=2,'rep'=2] {'var'}, dimensions={0}, use_global_device_ids=true | all-gather | bytes 983040 | tf_op jit(solution)/shard_map/all_gather | solution.py:36
  183.8 0.5 copy.101
  184.4 1.6 gather_fusion.3
  186.0 1.4 broadcast_select_fusion.3
  187.4 1.8 copy.166
  189.2 1.8 copy.165
  191.0 0.8 reduce-scatter.8.cloned.1.call-done
  191.7 1.0 add_convert_fusion.3
  192.7 1.9 all_gather.23
  194.7 0.1 copy.164
  194.8 6.1 %fusion = bf16[64,3,128,128]{2,3,1,0:T(8,128)(2,1)} fusion(bf16[1,64,3,12,128]{4,3,0,2,1:T(8,128)(2,1)S(1)} %bitcast.67, bf16[1,64,3,12,128]{4,3,0,2,1:T(8,128)(2,1)S(1)} %bitcast.69, bf16[1,64,3,12,128]{4,3,0,2,1:T(8,128)(2,1)S(1)} %bitcast.71, bf16[1,64,3,12,128]{4,3,0,2,1:T(8,128)(2,1)S(1)} %bitcast.74, bf16[1,64,12,128]{3,2,0,1:T(8,128)(2,1)S(1)} %bitcast.77, ...), kind=kOutput, calls=%fused_computation.9 | convolution fusion | flops 309854208 | bytes 9437184 | tf_op jit(solution)/shard_map/trsi,trksj->rkij/dot_general | solution.py:57
  200.9 152.0 %all-reduce.11.cloned.1.call-done = bf16[64,3,128,128]{2,3,1,0:T(8,128)(2,1)} async-done(((bf16[64,3,128,128]{2,3,1,0:T(8,128)(2,1)}), bf16[64,3,128,128]{2,3,1,0:T(8,128)(2,1)}) %all-reduce.11.cloned.1.call-update) | async-done | bytes 6291472 | tf_op jit(solution)/shard_map/psum | solution.py:60
  352.9 8.3 %multiply_convert_fusion = bf16[64,3,128,128]{2,3,1,0:T(8,128)(2,1)} fusion(bf16[64,3,128,128]{2,3,1,0:T(8,128)(2,1)} %all-reduce.11.cloned.1.call-done), kind=kLoop, calls=%fused_computation.8 | loop fusion | flops 9437184 | bytes 12582912 | tf_op jit(solution)/shard_map/convert_element_type | solution.py:61
  361.2 8.6 %copy.120 = bf16[64,3,128,128]{3,2,1,0:T(8,128)(2,1)} copy(bf16[64,3,128,128]{2,3,1,0:T(8,128)(2,1)} %multiply_convert_fusion) | data formatting | bytes 12582912 | tf_op jit(solution)/shard_map/convert_element_type | solution.py:61
  (27 shorter events, 0.2 us)
Async XLA Ops:
  7.4 33.3 %all-reduce.5.cloned.1.call-start = ((), (), s32[]{:S(2)}) async-start(), calls=%async_computation.3 | async-start | bytes 393216 | tf_op jit(solution)/shard_map/psum | solution.py:34
  11.5 5.4 %copy-start = (bf16[192,12,128]{2,1,0:T(8,128)(2,1)}, bf16[192,12,128]{2,1,0:T(8,128)(2,1)S(1)}, u32[]{:S(2)}) copy-start(bf16[192,12,128]{2,1,0:T(8,128)(2,1)S(1)} %broadcast_select_fusion.2) | copy-start | bytes 1769476
  17.6 59.1 %reduce-scatter.4.cloned.1.call-start = ((), (), s32[]{:S(2)}) async-start(), calls=%async_computation.6 | async-start | bytes 884736 | tf_op jit(solution)/shard_map/reduce_scatter | solution.py:45
  40.6 61.4 %all-reduce.7.cloned.1.call-start = ((), (), s32[]{:S(2)}) async-start(), calls=%async_computation.4 | async-start | bytes 393216 | tf_op jit(solution)/shard_map/psum | solution.py:34
  68.2 5.4 %copy-start.2 = (bf16[192,12,128]{2,1,0:T(8,128)(2,1)}, bf16[192,12,128]{2,1,0:T(8,128)(2,1)S(1)}, u32[]{:S(2)}) copy-start(bf16[192,12,128]{2,1,0:T(8,128)(2,1)S(1)} %broadcast_select_fusion.1) | copy-start | bytes 1769476
  74.4 59.6 %reduce-scatter.6.cloned.1.call-start = ((), (), s32[]{:S(2)}) async-start(), calls=%async_computation.7 | async-start | bytes 884736 | tf_op jit(solution)/shard_map/reduce_scatter | solution.py:45
  79.6 54.3 %copy-start.4 = (bf16[64,12,128]{2,0,1:T(8,128)(2,1)}, bf16[64,12,128]{2,0,1:T(8,128)(2,1)S(1)}, u32[]{:S(2)}) copy-start(bf16[64,12,128]{2,0,1:T(8,128)(2,1)S(1)} %all_gather.21) | copy-start | bytes 589828
  102.0 58.1 %all-reduce.9.cloned.1.call-start = ((), (), s32[]{:S(2)}) async-start(), calls=%async_computation.5 | async-start | bytes 393216 | tf_op jit(solution)/shard_map/psum | solution.py:34
  133.5 58.2 %reduce-scatter.8.cloned.1.call-start = ((), (), s32[]{:S(2)}) async-start(), calls=%async_computation.8 | async-start | bytes 884736 | tf_op jit(solution)/shard_map/reduce_scatter | solution.py:45
  136.8 5.3 %copy-start.5 = (bf16[64,12,128]{2,0,1:T(8,128)(2,1)}, bf16[64,12,128]{2,0,1:T(8,128)(2,1)S(1)}, u32[]{:S(2)}) copy-start(bf16[64,12,128]{2,0,1:T(8,128)(2,1)S(1)} %all_gather.22) | copy-start | bytes 589828
  142.3 17.0 %copy-start.6 = (bf16[1,64,12,128]{3,1,2,0:T(8,128)(2,1)S(1)}, bf16[1,64,12,128]{3,1,2,0:T(8,128)(2,1)}, u32[]{:S(2)}) copy-start(bf16[1,64,12,128]{3,1,2,0:T(8,128)(2,1)} %get-tuple-element.6) | copy-start | bytes 589828
  159.2 193.7 %all-reduce.11.cloned.1.call-start = ((), (), s32[]{:S(2)}) async-start(), calls=%async_computation.9 | async-start | bytes 12582912 | tf_op jit(solution)/shard_map/psum | solution.py:60
  183.8 11.0 %copy-start.1 = (bf16[192,12,128]{2,1,0:T(8,128)(2,1)S(1)}, bf16[192,12,128]{2,1,0:T(8,128)(2,1)}, u32[]{:S(2)}) copy-start(bf16[192,12,128]{2,1,0:T(8,128)(2,1)} %copy-done) | copy-start | bytes 1769476
  183.8 11.0 %copy-start.3 = (bf16[192,12,128]{2,1,0:T(8,128)(2,1)S(1)}, bf16[192,12,128]{2,1,0:T(8,128)(2,1)}, u32[]{:S(2)}) copy-start(bf16[192,12,128]{2,1,0:T(8,128)(2,1)} %copy-done.2) | copy-start | bytes 1769476
Sparse Core Ops, SparseCore 0:
  17.8 20.7 all-reduce.4
  74.5 18.5 all-reduce.6
  133.6 17.1 all-reduce.8
  201.1 151.8 all-reduce.10
Sparse Core Ops, SparseCore 1:
  40.7 36.0 reduce-scatter.3
  102.0 31.9 reduce-scatter.5
  159.3 32.4 reduce-scatter.7
where the time goes:
time: 379 us; the launch traced here: 377 us
  waiting for transfers between devices  156 us (41%)
  blocking collectives  76.5 us (20%)
  other arithmetic  64.3 us (17%)
  matrix products  37.7 us (10%)
  local copies, waits for them, and re-layouts  27.7 us (7%)
  between operations  15.1 us (4%)
    psum x1, waiting for transfers between devices, local(): lax.psum(estimate.astype(jnp.bfloat16), 'probe').astype(jnp.float32)  152 us
    all_gather x3, blocking collectives, local(): lax.all_gather(forward_own, 'var', axis=0, tiled=True)  70.7 us
    scatter-add x3, other arithmetic, local(): jax.ops.segment_sum(weighted, column_list, num_segments=blocks_all)  46.4 us
    dot_general x3, matrix products, local(): jnp.einsum('rkij,rksj->rsi', block_values, shaped, preferred_element_type...  15.8 us
    dot_general x3, matrix products, local(): jnp.einsum('rkij,rsi->rksj', block_values, panel_own, preferred_element_t...  15.7 us
    convert_element_type x1, local copies, waits for them, and re-layouts, local(): return (estimate / total_probes).astype(jnp.bfloat16)  8.61 us
    convert_element_type x1, other arithmetic, local(): return (estimate / total_probes).astype(jnp.bfloat16)  8.26 us
  transfers between devices with their start and end apart: 7, of which 4 were waited for; matrix products, arithmetic and copies ran while one was open for 25% of the time, Pallas kernels for 0%

commit v1 on v0

--- a/solution.py
+++ b/solution.py
@@ -57,7 +57,9 @@
     estimate = jnp.einsum(
         "trsi,trksj->rkij", left_panels, right_blocks, preferred_element_type=jnp.float32
     )
-    estimate = lax.psum(estimate.astype(jnp.bfloat16), "probe").astype(jnp.float32)
+    estimate = jnp.sum(lax.all_gather(estimate.astype(jnp.bfloat16), "probe"), axis=0).astype(
+        jnp.float32
+    )
     return (estimate / total_probes).astype(jnp.bfloat16)
 
 

time: 379 us -> 409 us (1.079)
  local copies, waits for them, and re-layouts: 27.7 us -> 45.1 us
  other arithmetic: 64.3 us -> 77.1 us
    psum x1 -> x0, waiting for transfers between devices: 152 us -> none  [local(): lax.psum(estimate.astype(jnp.bfloat16), 'probe').astype(jnp.float32)]
    all_gather x0 -> x1, waiting for transfers between devices: none -> 151 us  [local(): lax.all_gather(estimate.astype(jnp.bfloat16), 'probe')]
    reduce_sum x0 -> x1, other arithmetic: none -> 12.7 us  [local(): jnp.sum(lax.all_gather(estimate.astype(jnp.bfloat16), 'probe'), axis=0)]
    convert_element_type x0 -> x1, local copies, waits for them, and re-layouts: none -> 8.69 us  [local(): estimate.astype(jnp.bfloat16)]
    unnamed x15 -> x16, local copies, waits for them, and re-layouts: 0.8 us -> 9.47 us
  transfers between devices with their start and end apart: 7 -> 7, of which waited for: 4 -> 4; matrix products, arithmetic and copies ran while one was open for 25% -> 23% of each run, Pallas kernels for 0% -> 0%
where the time goes in v1:
time: 409 us; the launch traced here: 407 us
  waiting for transfers between devices  155 us (38%)
  other arithmetic  77.1 us (19%)
  blocking collectives  76.7 us (19%)
  local copies, waits for them, and re-layouts  45.1 us (11%)
  matrix products  37.7 us (9%)
  between operations  15.1 us (4%)
    all_gather x1, waiting for transfers between devices, local(): lax.all_gather(estimate.astype(jnp.bfloat16), 'probe')  151 us
    all_gather x3, blocking collectives, local(): lax.all_gather(forward_own, 'var', axis=0, tiled=True)  70.7 us
    scatter-add x3, other arithmetic, local(): jax.ops.segment_sum(weighted, column_list, num_segments=blocks_all)  46.4 us
    dot_general x3, matrix products, local(): jnp.einsum('rkij,rksj->rsi', block_values, shaped, preferred_element_type...  15.8 us
    dot_general x3, matrix products, local(): jnp.einsum('rkij,rsi->rksj', block_values, panel_own, preferred_element_t...  15.7 us
    reduce_sum x1, other arithmetic, local(): jnp.sum(lax.all_gather(estimate.astype(jnp.bfloat16), 'probe'), axis=0)  12.7 us
    unnamed x16, local copies, waits for them, and re-layouts  9.47 us
    convert_element_type x1, local copies, waits for them, and re-layouts, local(): estimate.astype(jnp.bfloat16)  8.69 us
  transfers between devices with their start and end apart: 7, of which 4 were waited for; matrix products, arithmetic and copies ran while one was open for 23% of the time, Pallas kernels for 0%

profile of v1, /device:TPU:0, one launch (start us, length us, event | category | flops | bytes accessed | tf_op | source)
XLA Modules:
  0.0 406.8 jit_solution(15794500455594584040)
XLA Ops:
  7.4 0.8 copy.92
  8.1 0.1 reshape.35
  8.3 1.6 convert_element_type.89
  9.9 0.5 copy.93
  10.4 0.8 gather_fusion
  11.2 0.3 broadcast_select_fusion.2
  11.5 5.4 %convolution_bitcast_fusion.2 = bf16[64,12,128]{2,1,0:T(8,128)(2,1)S(1)} fusion(bf16[64,3,12,128]{3,2,1,0:T(8,128)(2,1)S(1)} %bitcast.68, bf16[64,3,128,128]{3,2,1,0:T(8,128)(2,1)} %param.5), kind=kOutput, calls=%fused_computation.22 | convolution fusion | flops 75497472 | bytes 7077888 | tf_op jit(solution)/shard_map/rkij,rksj->rsi/dot_general | solution.py:31
  16.9 0.7 copy.170
  17.6 0.0 reduce-scatter.4.cloned.1.call-start
  17.7 0.7 dynamic-slice_bitcast_fusion.1
  18.4 5.1 %fusion.18 = f32[64,12,3,128]{3,1,2,0:T(8,128)} fusion(bf16[64,3,128,128]{3,2,1,0:T(8,128)(2,1)} %param.5, bf16[64,12,128,1]{2,0,1,3:T(8,128)(2,1)S(1)} %get-tuple-element.7), kind=kOutput, calls=%fused_computation.44 | convolution fusion | flops 75497472 | bytes 7667712 | tf_op jit(solution)/shard_map/rkij,rsi->rksj/dot_general | solution.py:39
  23.6 0.1 broadcast.14.clone.1
  23.7 15.5 %scatter_fusion = f32[256,12,128]{2,1,0:T(8,128)S(1)} fusion(f32[256,12,128]{2,1,0:T(8,128)S(1)} %broadcast.14.clone.1, s32[192]{0:T(256)S(1)} %reshape.35, f32[192,12,128]{2,1,0:T(8,128)} %bitcast.66), kind=kCustom, calls=%fused_computation.4 | custom fusion | flops 294912 | bytes 3539712 | tf_op jit(solution)/shard_map/scatter-add | solution.py:43
  39.2 1.4 copy.167
  40.7 1.0 add_convert_fusion.2
  41.7 24.9 %all_gather.24 = bf16[256,12,128]{2,0,1:T(8,128)(2,1)S(1)} all-gather(bf16[64,12,128]{2,0,1:T(8,128)(2,1)S(1)} %add_convert_fusion.2), channel_id=1, replica_groups=mesh['groups'=2,'var'=4,'probe'=2,'rep'=2] {'var'}, dimensions={0}, use_global_device_ids=true | all-gather | bytes 983040 | tf_op jit(solution)/shard_map/all_gather | solution.py:36
  66.6 0.5 copy.97
  67.2 0.8 gather_fusion.1
  68.0 0.3 broadcast_select_fusion.1
  68.2 5.4 %convolution_bitcast_fusion.1 = bf16[64,12,128]{2,1,0:T(8,128)(2,1)S(1)} fusion(bf16[64,3,12,128]{3,2,1,0:T(8,128)(2,1)S(1)} %bitcast.70, bf16[64,3,128,128]{3,2,1,0:T(8,128)(2,1)} %param.5), kind=kOutput, calls=%fused_computation.21 | convolution fusion | flops 75497472 | bytes 7077888 | tf_op jit(solution)/shard_map/rkij,rksj->rsi/dot_general | solution.py:31
  73.6 0.7 copy.169
  74.4 0.0 reduce-scatter.6.cloned.1.call-start
  74.5 2.3 reduce-scatter.4.cloned.1.call-done
  76.7 0.9 add_convert_fusion.5
  77.7 1.9 all_gather.27
  79.6 5.3 %fusion.16 = f32[64,12,3,128]{3,1,2,0:T(8,128)} fusion(bf16[64,3,128,128]{3,2,1,0:T(8,128)(2,1)} %param.5, bf16[64,12,128,1]{2,0,1,3:T(8,128)(2,1)S(1)} %bitcast.74), kind=kOutput, calls=%fused_computation.42 | convolution fusion | flops 75497472 | bytes 7667712 | tf_op jit(solution)/shard_map/rkij,rsi->rksj/dot_general | solution.py:39
  84.9 0.1 broadcast.14.clone
  85.1 15.5 %scatter_fusion.1 = f32[256,12,128]{2,1,0:T(8,128)S(1)} fusion(f32[256,12,128]{2,1,0:T(8,128)S(1)} %broadcast.14.clone, s32[192]{0:T(256)S(1)} %reshape.35, f32[192,12,128]{2,1,0:T(8,128)} %bitcast.67), kind=kCustom, calls=%fused_computation.5 | custom fusion | flops 294912 | bytes 3539712 | tf_op jit(solution)/shard_map/scatter-add | solution.py:43
  100.5 1.4 copy.166
  102.0 1.0 add_convert_fusion.1
  103.0 23.0 %all_gather.25 = bf16[256,12,128]{2,0,1:T(8,128)(2,1)S(1)} all-gather(bf16[64,12,128]{2,0,1:T(8,128)(2,1)S(1)} %add_convert_fusion.1), channel_id=1, replica_groups=mesh['groups'=2,'var'=4,'probe'=2,'rep'=2] {'var'}, dimensions={0}, use_global_device_ids=true | all-gather | bytes 983040 | tf_op jit(solution)/shard_map/all_gather | solution.py:36
  126.1 0.5 copy.101
  126.6 0.8 gather_fusion.2
  127.4 0.3 broadcast_select_fusion
  127.7 5.1 %convolution_bitcast_fusion = bf16[64,12,128]{2,1,0:T(8,128)(2,1)S(1)} fusion(bf16[64,3,12,128]{3,2,1,0:T(8,128)(2,1)S(1)} %bitcast.72, bf16[64,3,128,128]{3,2,1,0:T(8,128)(2,1)} %param.5), kind=kOutput, calls=%fused_computation.20 | convolution fusion | flops 75497472 | bytes 7077888 | tf_op jit(solution)/shard_map/rkij,rksj->rsi/dot_general | solution.py:31
  132.8 0.7 copy.168
  133.5 0.0 reduce-scatter.8.cloned.1.call-start
  133.6 0.4 reduce-scatter.6.cloned.1.call-done
  134.0 0.9 add_convert_fusion.4
  134.9 1.9 all_gather.28
  136.8 5.3 %fusion.14 = f32[64,12,3,128]{3,1,2,0:T(8,128)} fusion(bf16[64,3,128,128]{3,2,1,0:T(8,128)(2,1)} %param.5, bf16[64,12,128,1]{2,0,1,3:T(8,128)(2,1)S(1)} %bitcast.75), kind=kOutput, calls=%fused_computation.40 | convolution fusion | flops 75497472 | bytes 7667712 | tf_op jit(solution)/shard_map/rkij,rsi->rksj/dot_general | solution.py:39
  142.1 0.1 broadcast.14
  142.3 15.5 %scatter_fusion.2 = f32[256,12,128]{2,1,0:T(8,128)S(1)} fusion(f32[256,12,128]{2,1,0:T(8,128)S(1)} %broadcast.14, s32[192]{0:T(256)S(1)} %reshape.35, f32[192,12,128]{2,1,0:T(8,128)} %bitcast.65), kind=kCustom, calls=%fused_computation.6 | custom fusion | flops 294912 | bytes 3539712 | tf_op jit(solution)/shard_map/scatter-add | solution.py:43
  157.8 1.4 copy.165
  159.2 0.0 all-gather.3.cloned.1.call-start
  159.3 0.8 copy.123
  160.1 1.0 add_convert_fusion
  161.1 22.7 %all_gather.26 = bf16[256,12,128]{2,0,1:T(8,128)(2,1)S(1)} all-gather(bf16[64,12,128]{2,0,1:T(8,128)(2,1)S(1)} %add_convert_fusion), channel_id=1, replica_groups=mesh['groups'=2,'var'=4,'probe'=2,'rep'=2] {'var'}, dimensions={0}, use_global_device_ids=true | all-gather | bytes 983040 | tf_op jit(solution)/shard_map/all_gather | solution.py:36
  183.8 0.5 copy.105
  184.4 1.6 gather_fusion.3
  186.0 1.4 broadcast_select_fusion.3
  187.4 1.8 copy.173
  189.2 1.8 copy.172
  191.0 0.8 reduce-scatter.8.cloned.1.call-done
  191.7 1.0 add_convert_fusion.3
  192.7 2.2 all_gather.29
  194.9 0.1 copy.171
  195.0 6.1 %fusion = bf16[64,3,128,128]{2,3,1,0:T(8,128)(2,1)} fusion(bf16[1,64,3,12,128]{4,3,0,2,1:T(8,128)(2,1)S(1)} %bitcast.69, bf16[1,64,3,12,128]{4,3,0,2,1:T(8,128)(2,1)S(1)} %bitcast.71, bf16[1,64,3,12,128]{4,3,0,2,1:T(8,128)(2,1)S(1)} %bitcast.73, bf16[1,64,3,12,128]{4,3,0,2,1:T(8,128)(2,1)S(1)} %bitcast.76, bf16[1,64,12,128]{3,2,0,1:T(8,128)(2,1)S(1)} %bitcast.79, ...), kind=kOutput, calls=%fused_computation.9 | convolution fusion | flops 309854208 | bytes 9437184 | tf_op jit(solution)/shard_map/trsi,trksj->rkij/dot_general | solution.py:57
  201.1 8.7 %copy.124 = bf16[64,3,128,128]{3,2,1,0:T(8,128)(2,1)} copy(bf16[64,3,128,128]{2,3,1,0:T(8,128)(2,1)} %fusion) | data formatting | bytes 12582912 | tf_op jit(solution)/shard_map/convert_element_type | solution.py:60
  209.9 151.3 %all-gather.3.cloned.1.call-done = bf16[128,3,128,128]{3,2,1,0:T(8,128)(2,1)} async-done(((bf16[64,3,128,128]{3,2,1,0:T(8,128)(2,1)}), bf16[128,3,128,128]{3,2,1,0:T(8,128)(2,1)}) %all-gather.3.cloned.1.call-update) | async-done | bytes 12582928 | tf_op jit(solution)/shard_map/all_gather | solution.py:60
  361.2 12.7 %reduce_sum.12 = bf16[64,3,128,128]{3,2,1,0:T(8,128)(2,1)} reduce(bf16[2,64,3,128,128]{4,3,2,1,0:T(8,128)(2,1)} %bitcast.64, bf16[]{:T(256)} %constant.50.clone.1), dimensions={0}, to_apply=%region_9.11 | reduce | flops 3145728 | bytes 18874370 | tf_op jit(solution)/shard_map/reduce_sum | solution.py:60
  373.9 8.7 %copy.149 = bf16[64,3,128,128]{2,3,1,0:T(8,128)(2,1)} copy(bf16[64,3,128,128]{3,2,1,0:T(8,128)(2,1)} %reduce_sum.12) | data formatting | bytes 12582912
  382.6 8.3 %multiply_convert_fusion = bf16[64,3,128,128]{2,3,1,0:T(8,128)(2,1)} fusion(bf16[64,3,128,128]{2,3,1,0:T(8,128)(2,1)} %copy.149), kind=kLoop, calls=%fused_computation.8 | loop fusion | flops 9437184 | bytes 12582912 | tf_op jit(solution)/shard_map/convert_element_type | solution.py:63
  390.8 8.6 %copy.126 = bf16[64,3,128,128]{3,2,1,0:T(8,128)(2,1)} copy(bf16[64,3,128,128]{2,3,1,0:T(8,128)(2,1)} %multiply_convert_fusion) | data formatting | bytes 12582912 | tf_op jit(solution)/shard_map/convert_element_type | solution.py:63
  (30 shorter events, 0.3 us)
Async XLA Ops:
  7.4 33.3 %all-reduce.4.cloned.1.call-start = ((), (), s32[]{:S(2)}) async-start(), calls=%async_computation.3 | async-start | bytes 393216 | tf_op jit(solution)/shard_map/psum | solution.py:34
  11.5 5.4 %copy-start = (bf16[192,12,128]{2,1,0:T(8,128)(2,1)}, bf16[192,12,128]{2,1,0:T(8,128)(2,1)S(1)}, u32[]{:S(2)}) copy-start(bf16[192,12,128]{2,1,0:T(8,128)(2,1)S(1)} %broadcast_select_fusion.2) | copy-start | bytes 1769476
  17.6 59.1 %reduce-scatter.4.cloned.1.call-start = ((), (), s32[]{:S(2)}) async-start(), calls=%async_computation.6 | async-start | bytes 884736 | tf_op jit(solution)/shard_map/reduce_scatter | solution.py:45
  40.6 61.4 %all-reduce.6.cloned.1.call-start = ((), (), s32[]{:S(2)}) async-start(), calls=%async_computation.4 | async-start | bytes 393216 | tf_op jit(solution)/shard_map/psum | solution.py:34
  68.2 5.4 %copy-start.2 = (bf16[192,12,128]{2,1,0:T(8,128)(2,1)}, bf16[192,12,128]{2,1,0:T(8,128)(2,1)S(1)}, u32[]{:S(2)}) copy-start(bf16[192,12,128]{2,1,0:T(8,128)(2,1)S(1)} %broadcast_select_fusion.1) | copy-start | bytes 1769476
  74.4 59.6 %reduce-scatter.6.cloned.1.call-start = ((), (), s32[]{:S(2)}) async-start(), calls=%async_computation.7 | async-start | bytes 884736 | tf_op jit(solution)/shard_map/reduce_scatter | solution.py:45
  79.6 54.3 %copy-start.4 = (bf16[64,12,128]{2,0,1:T(8,128)(2,1)}, bf16[64,12,128]{2,0,1:T(8,128)(2,1)S(1)}, u32[]{:S(2)}) copy-start(bf16[64,12,128]{2,0,1:T(8,128)(2,1)S(1)} %all_gather.27) | copy-start | bytes 589828
  102.0 58.1 %all-reduce.8.cloned.1.call-start = ((), (), s32[]{:S(2)}) async-start(), calls=%async_computation.5 | async-start | bytes 393216 | tf_op jit(solution)/shard_map/psum | solution.py:34
  133.5 58.2 %reduce-scatter.8.cloned.1.call-start = ((), (), s32[]{:S(2)}) async-start(), calls=%async_computation.8 | async-start | bytes 884736 | tf_op jit(solution)/shard_map/reduce_scatter | solution.py:45
  136.8 5.3 %copy-start.5 = (bf16[64,12,128]{2,0,1:T(8,128)(2,1)}, bf16[64,12,128]{2,0,1:T(8,128)(2,1)S(1)}, u32[]{:S(2)}) copy-start(bf16[64,12,128]{2,0,1:T(8,128)(2,1)S(1)} %all_gather.28) | copy-start | bytes 589828
  142.3 17.0 %copy-start.6 = (bf16[1,64,12,128]{3,1,2,0:T(8,128)(2,1)S(1)}, bf16[1,64,12,128]{3,1,2,0:T(8,128)(2,1)}, u32[]{:S(2)}) copy-start(bf16[1,64,12,128]{3,1,2,0:T(8,128)(2,1)} %get-tuple-element.6) | copy-start | bytes 589828
  159.2 202.0 %all-gather.3.cloned.1.call-start = ((), (), s32[]{:S(2)}) async-start(), calls=%async_computation.9 | async-start | bytes 18874368 | tf_op jit(solution)/shard_map/all_gather | solution.py:60
  183.8 11.2 %copy-start.1 = (bf16[192,12,128]{2,1,0:T(8,128)(2,1)S(1)}, bf16[192,12,128]{2,1,0:T(8,128)(2,1)}, u32[]{:S(2)}) copy-start(bf16[192,12,128]{2,1,0:T(8,128)(2,1)} %copy-done) | copy-start | bytes 1769476
  183.8 11.2 %copy-start.3 = (bf16[192,12,128]{2,1,0:T(8,128)(2,1)S(1)}, bf16[192,12,128]{2,1,0:T(8,128)(2,1)}, u32[]{:S(2)}) copy-start(bf16[192,12,128]{2,1,0:T(8,128)(2,1)} %copy-done.2) | copy-start | bytes 1769476
Sparse Core Ops, SparseCore 0:
  17.8 20.7 all-reduce.3
  74.5 18.5 all-reduce.5
  133.6 17.1 all-reduce.7
  210.0 151.1 all-gather.2
Sparse Core Ops, SparseCore 1:
  40.7 36.0 reduce-scatter.3
  102.0 31.9 reduce-scatter.5
  159.3 32.4 reduce-scatter.7
